TPU v7x, 32 devices: a whole 2x2x4 slice. The times are simulated.
32 devices in a mesh: fsdp: 8 (over y, x, core), tensor: 4 (over z).
Axes of the slice: x: 2, y: 2, z: 4, core: 2. Of those that a mesh axis runs over, the one named last changes fastest.
Arguments:
- hidden: bfloat16 [4096, 2048], P(('fsdp', 'tensor')), may hold values from -6 to 6
- cotangent: bfloat16 [4096, 2048], P(('fsdp', 'tensor')), may hold values from -6 to 6
- seq_lengths: int32 [8, 3], P('fsdp'), may hold values from 1 to 256, 512 in all within a row
- pack_order: int32 [8, 3], P('fsdp'), may hold values from 0 to 2, each once within a row
- norm_gain: bfloat16 [2048], P(('fsdp', 'tensor')), may hold values from 0.099609375 to 1.8984375
- w_in: bfloat16 [2, 4096, 2048], P(None, ('fsdp', 'tensor')), may hold values from -0.125 to 0.125
- conv_weight: bfloat16 [4096, 4], P(('fsdp', 'tensor')), may hold values from -3 to 3
- conv_bias: bfloat16 [4096], P(('fsdp', 'tensor')), may hold values from -3 to 3
- w_xproj: bfloat16 [4096, 160], P(('fsdp', 'tensor')), may hold values from -0.1875 to 0.1875
- w_dt: bfloat16 [4096, 128], P(('fsdp', 'tensor')), may hold values from -0.5 to 0.5
- dt_bias: bfloat16 [4096], P(('fsdp', 'tensor')), may hold values from -7 to -2
- a_log: bfloat16 [4096, 16], P(('fsdp', 'tensor')), may hold values from -1 to 2.6875
- d_skip: bfloat16 [4096], P(('fsdp', 'tensor')), may hold values from 0.099609375 to 1.8984375
- w_out: bfloat16 [4096, 2048], P(('fsdp', 'tensor')), may hold values from -0.1875 to 0.1875
Outputs:
- output: bfloat16 [4096, 2048], P(('fsdp', 'tensor'))
- grad_hidden: float32 [4096, 2048], P(('fsdp', 'tensor'))
- grad_norm_gain: float32 [2048], P(('fsdp', 'tensor'))
- grad_w_in: float32 [2, 4096, 2048], P(None, ('fsdp', 'tensor'))
- grad_conv_weight: float32 [4096, 4], P(('fsdp', 'tensor'))
- grad_conv_bias: float32 [4096], P(('fsdp', 'tensor'))
- grad_w_xproj: float32 [4096, 160], P(('fsdp', 'tensor'))
- grad_w_dt: float32 [4096, 128], P(('fsdp', 'tensor'))
- grad_dt_bias: float32 [4096], P(('fsdp', 'tensor'))
- grad_a_log: float32 [4096, 16], P(('fsdp', 'tensor'))
- grad_d_skip: float32 [4096], P(('fsdp', 'tensor'))
- grad_w_out: float32 [4096, 2048], P(('fsdp', 'tensor'))
Inputs may be any that keep to these rules, and one draw needn't show every extreme that they name: `seq_lengths`: each row holds the lengths of the 3 sequences of one token group; they sum to 512 and the largest of each row is exactly 256. `pack_order`: each row is a permutation of 0 to 2: the sequence packed into each slot.
All inputs are finite; a program needn't handle non-finite values.
Results may differ from a plain program's by a relative error of at most 0.012.
Values may be sent and summed in bfloat16 or wider, within the bound.
No kernel may reach another device: no remote copies, remote signals or barrier semaphores. Data moves between devices by JAX's collectives and lax.ppermute only.
A program may use at most 320 MiB of HBM per device.

v0:
```python
import math
import jax
import jax.numpy as jnp
from jax import lax
from jax.sharding import PartitionSpec as P

EPSILON = 1e-05


def normalize(values, scales):
    factor = lax.rsqrt(jnp.mean(values * values, axis=1, keepdims=True) + EPSILON)
    return values * factor * scales[None, :]


def distances(lengths, pack_rows, row_count):
    slot_count = lengths.shape[0]
    picks = pack_rows[:, None] == jnp.arange(slot_count, dtype=jnp.int32)[None, :]
    packed = jnp.sum(jnp.where(picks, lengths[None, :], 0), axis=1)
    starts = jnp.cumsum(packed) - packed
    positions = jnp.arange(row_count, dtype=jnp.int32)
    latest = jnp.max(jnp.where(starts[None, :] <= positions[:, None], starts[None, :], 0), axis=1)
    return positions - latest


def convolve(signal, weights, biases, offsets):
    kernel_taps = weights.shape[1]
    result = biases[None, :] + weights[:, kernel_taps - 1][None, :] * signal
    for lag_index in range(1, kernel_taps):
        shifted = jnp.concatenate(
            [jnp.zeros((lag_index, signal.shape[1]), jnp.float32), signal[:-lag_index]], axis=0
        )
        in_sequence = (offsets >= lag_index).astype(jnp.float32)[:, None]
        result = result + weights[:, kernel_taps - 1 - lag_index][None, :] * shifted * in_sequence
    return result


def block_scan(carried, step_sizes, inputs, b_in, c_out, decays, keep_mask):
    row_count = step_sizes.shape[0]
    stretch_len = math.gcd(row_count, 16)
    stretches = row_count // stretch_len
    channels = step_sizes.shape[1]
    state_cols = decays.shape[1]
    factors = jnp.exp(step_sizes[:, :, None] * decays[None, :, :]) * keep_mask[:, None, None]
    drives = (step_sizes * inputs)[:, :, None] * b_in[:, None, :]
    factors = factors.reshape(stretches, stretch_len, channels, state_cols)
    drives = drives.reshape(stretches, stretch_len, channels, state_cols)
    running = drives[:, 0]
    product = factors[:, 0]
    running_list = [running]
    product_list = [product]
    for offset in range(1, stretch_len):
        running = factors[:, offset] * running + drives[:, offset]
        product = factors[:, offset] * product
        running_list.append(running)
        product_list.append(product)
    running_all = jnp.stack(running_list, axis=1)
    product_all = jnp.stack(product_list, axis=1)

    def carry_step(current, members):
        return (members[0] * current + members[1], current)

    closing, entering = lax.scan(carry_step, carried, (product_all[:, -1], running_all[:, -1]))
    states = running_all + product_all * entering[:, None]
    states = states.reshape(row_count, channels, state_cols)
    return (closing, jnp.sum(states * c_out[:, None, :], axis=2))


def selective(step_sizes, inputs, b_in, c_out, decays, keep_mask, block_len):
    row_count = step_sizes.shape[0]
    blocks = row_count // block_len

    def block_step(carried, pieces):
        return block_scan(carried, pieces[0], pieces[1], pieces[2], pieces[3], decays, pieces[4])

    pieces = (
        step_sizes.reshape(blocks, block_len, -1),
        inputs.reshape(blocks, block_len, -1),
        b_in.reshape(blocks, block_len, -1),
        c_out.reshape(blocks, block_len, -1),
        keep_mask.reshape(blocks, block_len),
    )
    initial = jnp.zeros((step_sizes.shape[1], decays.shape[1]), jnp.float32)
    _, outputs = lax.scan(jax.checkpoint(block_step), initial, pieces)
    return outputs.reshape(row_count, -1)


def mix_states(
    proj, b_in, c_out, inner, gate_in, step_bias, log_rates, skip_scale, keep_mask, block_len
):
    step_sizes = jax.nn.softplus(proj + step_bias[None, :])
    decays = -jnp.exp(log_rates)
    scanned = selective(step_sizes, inner, b_in, c_out, decays, keep_mask, block_len)
    return (scanned + skip_scale[None, :] * inner) * jax.nn.silu(gate_in)


def shards(
    hidden,
    cotangent,
    seq_lengths,
    pack_order,
    norm_gain,
    w_in,
    conv_weight,
    conv_bias,
    w_xproj,
    w_dt,
    dt_bias,
    a_log,
    d_skip,
    w_out,
):
    f32 = jnp.float32
    bf16 = jnp.bfloat16
    n_fsdp = lax.axis_size("fsdp")
    n_tensor = lax.axis_size("tensor")
    tok_rows = hidden.shape[0]
    group_rows = tok_rows * n_tensor
    rank_cols = w_dt.shape[1]
    state_cols = a_log.shape[1]
    block_len = math.gcd(group_rows, 256)
    gathered = (
        lax.all_gather(w_in, "fsdp", axis=1, tiled=True),
        lax.all_gather(conv_weight, "fsdp", axis=0, tiled=True),
        lax.all_gather(conv_bias, "fsdp", axis=0, tiled=True),
        lax.all_gather(w_xproj, "fsdp", axis=0, tiled=True),
        lax.all_gather(w_dt, "fsdp", axis=0, tiled=True),
        lax.all_gather(dt_bias, "fsdp", axis=0, tiled=True),
        lax.all_gather(a_log, "fsdp", axis=0, tiled=True),
        lax.all_gather(d_skip, "fsdp", axis=0, tiled=True),
        lax.all_gather(w_out, "fsdp", axis=0, tiled=True),
        lax.all_gather(norm_gain, "fsdp", axis=0, tiled=True),
    )
    w_in_t, conv_w_t, conv_b_t, w_x_t, w_dt_t, dt_b_t, a_log_t, d_skip_t, w_out_t, gain_fsdp = (
        gathered
    )
    rows_all, gain_tensor = (
        lax.all_gather(hidden, "tensor", axis=0, tiled=True),
        lax.all_gather(gain_fsdp, "tensor", axis=0, tiled=True),
    )
    gain_full = gain_tensor.reshape(n_tensor, n_fsdp, -1).transpose(1, 0, 2).reshape(-1).astype(f32)
    offsets = distances(seq_lengths[0], pack_order[0], group_rows)
    keep_mask = (offsets > 0).astype(f32)
    row_values = rows_all.astype(f32)
    normed = normalize(row_values, gain_full).astype(bf16)
    xz_all = jnp.einsum("gd,hcd->ghc", normed, w_in_t, preferred_element_type=f32)
    signal = xz_all[:, 0]
    gate_in = xz_all[:, 1]
    inner, front_back = jax.vjp(
        lambda signal_in, taps_in, biases_in: jax.nn.silu(
            convolve(signal_in, taps_in, biases_in, offsets)
        ),
        signal,
        conv_w_t.astype(f32),
        conv_b_t.astype(f32),
    )
    inner_low = inner.astype(bf16)
    pieces_x = jnp.dot(inner_low, w_x_t, preferred_element_type=f32)
    mixed = lax.psum(pieces_x, "tensor")
    step_in = mixed[:, :rank_cols].astype(bf16)
    b_in = mixed[:, rank_cols : rank_cols + state_cols]
    c_out = mixed[:, rank_cols + state_cols :]
    proj = jnp.einsum("gr,cr->gc", step_in, w_dt_t, preferred_element_type=f32)
    gated, mixer_back = jax.vjp(
        lambda proj_in, b_part, c_part, inner_in, gate_part, bias_part, rates_part, skip_part: mix_states(
            proj_in,
            b_part,
            c_part,
            inner_in,
            gate_part,
            bias_part,
            rates_part,
            skip_part,
            keep_mask,
            block_len,
        ),
        proj,
        b_in,
        c_out,
        inner_low.astype(f32),
        gate_in,
        dt_b_t.astype(f32),
        a_log_t.astype(f32),
        d_skip_t.astype(f32),
    )
    gated_low = gated.astype(bf16)
    branch = lax.psum_scatter(
        jnp.dot(gated_low, w_out_t, preferred_element_type=f32),
        "tensor",
        scatter_dimension=0,
        tiled=True,
    )
    output = (hidden.astype(f32) + branch).astype(bf16)
    cot_all = lax.all_gather(cotangent, "tensor", axis=0, tiled=True)
    grad_gated = (
        jnp.einsum("gd,cd->gc", cot_all, w_out_t, preferred_element_type=f32)
        .astype(bf16)
        .astype(f32)
    )
    out_grad = jnp.einsum("gc,gd->cd", gated_low, cot_all, preferred_element_type=f32)
    g_proj, g_b, g_c, g_inner_scan, g_gate, g_dt_bias, g_a_log, g_d_skip = mixer_back(grad_gated)
    g_proj_low = g_proj.astype(bf16)
    g_step = jnp.dot(g_proj_low, w_dt_t, preferred_element_type=f32)
    w_dt_grad = jnp.einsum("gc,gr->cr", g_proj_low, step_in, preferred_element_type=f32)
    mixed_grad = lax.psum(jnp.concatenate([g_step, g_b, g_c], axis=1), "tensor")
    mixed_low = mixed_grad.astype(bf16)
    g_inner = g_inner_scan + jnp.einsum("gk,ck->gc", mixed_low, w_x_t, preferred_element_type=f32)
    w_x_grad = jnp.einsum("gc,gk->ck", inner_low, mixed_low, preferred_element_type=f32)
    g_signal, g_conv_w, g_conv_b = front_back(g_inner)
    g_xz = jnp.stack([g_signal, g_gate], axis=1).astype(bf16)
    w_in_grad = jnp.einsum("ghc,gd->hcd", g_xz, normed, preferred_element_type=f32)
    g_normed = jnp.einsum("ghc,hcd->gd", g_xz, w_in_t, preferred_element_type=f32)
    gain_term = jax.vjp(lambda scales: normalize(row_values, scales), gain_full)[1](g_normed)[0]
    gain_term = gain_term.reshape(n_fsdp, n_tensor, -1).transpose(1, 0, 2).reshape(-1)
    g_norm_own, gain_part = (
        lax.psum_scatter(g_normed, "tensor", scatter_dimension=0, tiled=True),
        lax.psum_scatter(gain_term, "tensor", scatter_dimension=0, tiled=True),
    )
    norm_back = jax.vjp(lambda own_values: normalize(own_values, gain_full), hidden.astype(f32))[1]
    grad_hidden = cotangent.astype(f32) + norm_back(g_norm_own)[0]
    results = (
        lax.psum_scatter(w_in_grad, "fsdp", scatter_dimension=1, tiled=True),
        lax.psum_scatter(g_conv_w, "fsdp", scatter_dimension=0, tiled=True),
        lax.psum_scatter(g_conv_b, "fsdp", scatter_dimension=0, tiled=True),
        lax.psum_scatter(w_x_grad, "fsdp", scatter_dimension=0, tiled=True),
        lax.psum_scatter(w_dt_grad, "fsdp", scatter_dimension=0, tiled=True),
        lax.psum_scatter(g_dt_bias, "fsdp", scatter_dimension=0, tiled=True),
        lax.psum_scatter(g_a_log, "fsdp", scatter_dimension=0, tiled=True),
        lax.psum_scatter(g_d_skip, "fsdp", scatter_dimension=0, tiled=True),
        lax.psum_scatter(out_grad, "fsdp", scatter_dimension=0, tiled=True),
        lax.psum_scatter(gain_part, "fsdp", scatter_dimension=0, tiled=True),
    )
    return (
        output,
        grad_hidden,
        results[9],
        results[0],
        results[1],
        results[2],
        results[3],
        results[4],
        results[5],
        results[6],
        results[7],
        results[8],
    )


def solution(mesh):
    placed = (
        P(("fsdp", "tensor"), None),
        P(("fsdp", "tensor"), None),
        P("fsdp", None),
        P("fsdp", None),
        P(("fsdp", "tensor")),
        P(None, ("fsdp", "tensor"), None),
        P(("fsdp", "tensor"), None),
        P(("fsdp", "tensor")),
        P(("fsdp", "tensor"), None),
        P(("fsdp", "tensor"), None),
        P(("fsdp", "tensor")),
        P(("fsdp", "tensor"), None),
        P(("fsdp", "tensor")),
        P(("fsdp", "tensor"), None),
    )
    return jax.shard_map(
        shards,
        mesh=mesh,
        in_specs=placed,
        out_specs=(
            P(("fsdp", "tensor"), None),
            P(("fsdp", "tensor"), None),
            P(("fsdp", "tensor")),
            P(None, ("fsdp", "tensor"), None),
            P(("fsdp", "tensor"), None),
            P(("fsdp", "tensor")),
            P(("fsdp", "tensor"), None),
            P(("fsdp", "tensor"), None),
            P(("fsdp", "tensor")),
            P(("fsdp", "tensor"), None),
            P(("fsdp", "tensor")),
            P(("fsdp", "tensor"), None),
        ),
        check_vma=False,
    )
```

profile of v0, /device:TPU:0, one launch (start us, length us, event | category | flops | bytes accessed | tf_op | source)
XLA Modules:
  0.0 1662.1 jit_solution(14647917128028557112)
XLA Ops:
  12.9 15.5 all-reduce.59
  28.4 12.4 all-gather.1
  41.0 7.7 all-gather
  49.8 8.9 all_gather.40
  58.8 8.8 all_gather.45
  70.0 43.4 %all-gather.11.cloned.1.call-done = bf16[2,1024,2048]{2,1,0:T(8,128)(2,1)} async-done(((bf16[2,128,2048]{2,1,0:T(8,128)(2,1)}), bf16[2,1024,2048]{2,1,0:T(8,128)(2,1)}) %all-gather.11.cloned.1.call-update) | async-done | bytes 8388624 | tf_op jit(solution)/shard_map/all_gather | solution.py:122
  113.4 7.7 fusion.64
  125.2 35.7 %all-gather.15.cloned.1.call-done = bf16[512,2048]{1,0:T(8,128)(2,1)} async-done(((bf16[128,2048]{1,0:T(8,128)(2,1)}), bf16[512,2048]{1,0:T(8,128)(2,1)}) %all-gather.15.cloned.1.call-update) | async-done | bytes 2097168 | tf_op jit(solution)/shard_map/all_gather | solution.py:193
  160.9 37.2 %all-gather.13.cloned.1.call-done = bf16[1024,2048]{1,0:T(8,128)(2,1)} async-done(((bf16[128,2048]{1,0:T(8,128)(2,1)}), bf16[1024,2048]{1,0:T(8,128)(2,1)}) %all-gather.13.cloned.1.call-update) | async-done | bytes 4194320 | tf_op jit(solution)/shard_map/all_gather | solution.py:130
  198.2 12.5 multiply_reduce_fusion.6
  212.6 8.7 all-gather.2
  221.3 7.8 all-gather.3
  229.7 8.8 all_gather.48
  238.5 9.3 all_gather.46
  255.4 242.1 %while.116 = (s32[]{:T(128)}, f32[1024,16]{0,1:T(8,128)S(1)}, f32[2,256,1024]{2,1,0:T(8,128)}, f32[2,1024,16]{1,2,0:T(8,128)}, f32[2,256,1024]{2,1,0:T(8,128)}, ...) while((s32[]{:T(128)}, f32[1024,16]{0,1:T(8,128)S(1)}, ...), condition=%wide.region_9.10_spmd, body=%wide.region_5.9_spmd.sunk | while | flops 52199424 | bytes 568369280 | solution.py:83
  282.1 5.8 copy-done.3
  290.0 8.5 broadcast_multiply_fusion.10
  334.5 6.3 bitcast_add_fusion.23
  342.7 24.7 %while.120 = (s32[]{:T(128)}, f32[1024,16]{0,1:T(8,128)S(1)}, f32[16,1024,16]{1,2,0:T(8,128)}, f32[16,1024,16]{1,2,0:T(8,128)}, f32[16,1024,16]{1,2,0:T(8,128)}, /*index=5*/s32[]{:T(128)}) while((s32[]{:T(128)}, f32[1024,16]{0,1:T(8,128)S(1)}, f32[16,1024,16]{1,2,0:T(8,128)}, f32[16,1024,16]{1,2,0:T(8,128)}, f32[16,1024,16]{1,2,0:T(8,128)}, ...), condition=%wide.region_7.7_spmd, body=%wide.region_6.6_spmd.sunk | while | flops 32770 | bytes 393801 | solution.py:62
  367.7 12.8 multiply_reduce_fusion.15
  396.4 5.8 copy-done.3
  404.3 8.5 broadcast_multiply_fusion.10
  448.8 6.3 bitcast_add_fusion.23
  457.0 24.7 %while.120 = (s32[]{:T(128)}, f32[1024,16]{0,1:T(8,128)S(1)}, f32[16,1024,16]{1,2,0:T(8,128)}, f32[16,1024,16]{1,2,0:T(8,128)}, f32[16,1024,16]{1,2,0:T(8,128)}, /*index=5*/s32[]{:T(128)}) while((s32[]{:T(128)}, f32[1024,16]{0,1:T(8,128)S(1)}, f32[16,1024,16]{1,2,0:T(8,128)}, f32[16,1024,16]{1,2,0:T(8,128)}, f32[16,1024,16]{1,2,0:T(8,128)}, ...), condition=%wide.region_7.7_spmd, body=%wide.region_6.6_spmd.sunk | while | flops 32770 | bytes 393801 | solution.py:62
  482.0 12.8 multiply_reduce_fusion.15
  502.0 609.0 %while.119 = (s32[]{:T(128)}, f32[1024,16]{0,1:T(8,128)}, f32[1024,16]{0,1:T(8,128)S(1)}, f32[2,256,1024]{2,1,0:T(8,128)}, f32[2,256,1024]{2,1,0:T(8,128)}, /*in...) while((s32[]{:T(128)}, f32[1024,16]{0,1:T(8,128)}, ...), condition=%wide.region_22.23_spmd.clone, body=%wide.region_11.22_spmd.clone.sunk | while | flops 338518016 | bytes 1045472448 | solution.py:83
  533.5 7.0 broadcast_multiply_fusion.11
  541.3 6.5 fusion.145
  547.8 13.2 bitcast_add_fusion.24
  578.4 9.7 fusion.146
  634.5 15.0 while.121
  651.6 13.3 multiply_reduce_fusion.16
  666.1 24.8 %while.122 = (s32[]{:T(128)}, f32[1024,16]{0,1:T(8,128)S(1)}, f32[16,1024,16]{1,2,0:T(8,128)S(1)}, f32[16,1024,16]{1,2,0:T(8,128)}, f32[16,1024,16]{1,2,0:T(8,12...) while((s32[]{:T(128)}, f32[1024,16]{0,1:T(8,128)S(1)}, ...), condition=%wide.region_16.16_spmd, body=%wide.region_15.15_spmd.sunk | while | flops 49155 | bytes 524401 | solution.py:62
  690.9 7.5 multiply_add_fusion.26
  698.5 5.7 copy-done.2
  705.7 15.5 slice_add_fusion.81
  721.4 11.0 multiply_reduce_fusion.18
  793.8 14.9 multiply_reduce_fusion.17
  822.5 7.0 broadcast_multiply_fusion.11
  830.3 6.5 fusion.145
  836.9 13.2 bitcast_add_fusion.24
  867.5 9.7 fusion.146
  923.5 15.0 while.121
  940.7 13.3 multiply_reduce_fusion.16
  955.2 24.8 %while.122 = (s32[]{:T(128)}, f32[1024,16]{0,1:T(8,128)S(1)}, f32[16,1024,16]{1,2,0:T(8,128)S(1)}, f32[16,1024,16]{1,2,0:T(8,128)}, f32[16,1024,16]{1,2,0:T(8,12...) while((s32[]{:T(128)}, f32[1024,16]{0,1:T(8,128)S(1)}, ...), condition=%wide.region_16.16_spmd, body=%wide.region_15.15_spmd.sunk | while | flops 49155 | bytes 524401 | solution.py:62
  980.0 7.5 multiply_add_fusion.26
  994.8 15.5 slice_add_fusion.81
  1010.4 11.0 multiply_reduce_fusion.18
  1082.9 14.9 multiply_reduce_fusion.17
  1118.0 25.8 %all-reduce.70 = bf16[512,160]{0,1:T(8,128)(2,1)S(1)} all-reduce(f32[512,160]{0,1:T(8,128)S(1)} %pad_maximum_fusion.3), channel_id=1, replica_groups=mesh['fsdp'=8,'tensor'=4] {'tensor'}, use_global_device_ids=true, to_apply=%region_23.24 | all-reduce | flops 81920 | bytes 491520 | tf_op jit(solution)/shard_map/psum | solution.py:204
  1143.9 6.2 multiply_reduce_fusion.10
  1156.8 11.3 fusion.49
  1168.2 6.8 fusion.95
  1178.7 7.8 fusion.96
  1186.6 9.5 fusion.62
  1199.4 9.7 all-reduce.60
  1209.2 24.0 %all-reduce.65 = (f32[512]{0:T(512)S(1)}, f32[1024]{0:T(1024)S(1)}, f32[1024]{0:T(1024)S(1)}, f32[1024]{0:T(1024)S(1)}) all-reduce(f32[512]{0:T(512)S(1)} %dynamic-slice.2, f32[1024]{0:T(1024)S(1)} %get-tuple-element.866, f32[1024]{0:T(1024)S(1)} %get-tuple-element.1057, ...), channel_id=5, replica_groups=mesh['fsdp'=8,'tensor'=4] {'fsdp'}, use_global_device_ids=true, to_apply=%region_29.30.clone | all-reduce | flops 3584 | bytes 28672
  1236.9 31.1 %reduce-scatter.13.cloned.1.call-done = f32[128,2048]{1,0:T(8,128)} async-done(((f32[512,2048]{1,0:T(8,128)}), f32[128,2048]{1,0:T(8,128)}) %reduce-scatter.13.cloned.1.call-update) | async-done | bytes 1048592 | tf_op jit(solution)/shard_map/reduce_scatter | solution.py:215
  1269.6 78.0 %reduce-scatter.11.cloned.1.call-done = f32[128,2048]{1,0:T(8,128)} async-done(((f32[512,2048]{1,0:T(8,128)}), f32[128,2048]{1,0:T(8,128)}) %reduce-scatter.11.cloned.1.call-update) | async-done | bytes 1048592 | tf_op jit(solution)/shard_map/reduce_scatter | solution.py:186
  1350.6 32.8 %reduce-scatter.21.cloned.1.call-done = f32[128,16]{0,1:T(8,128)} async-done(((f32[1024,16]{0,1:T(8,128)}), f32[128,16]{0,1:T(8,128)}) %reduce-scatter.21.cloned.1.call-update) | async-done | bytes 8208 | tf_op jit(solution)/shard_map/reduce_scatter | solution.py:227
  1383.4 37.7 %reduce-scatter.19.cloned.1.call-done = f32[128,128]{1,0:T(8,128)} async-done(((f32[1024,128]{1,0:T(8,128)}), f32[128,128]{1,0:T(8,128)}) %reduce-scatter.19.cloned.1.call-update) | async-done | bytes 65552 | tf_op jit(solution)/shard_map/reduce_scatter | solution.py:225
  1421.0 38.6 %reduce-scatter.17.cloned.1.call-done = f32[128,160]{0,1:T(8,128)} async-done(((f32[1024,160]{0,1:T(8,128)}), f32[128,160]{0,1:T(8,128)}) %reduce-scatter.17.cloned.1.call-update) | async-done | bytes 81936 | tf_op jit(solution)/shard_map/reduce_scatter | solution.py:224
  1459.6 75.6 %reduce-scatter.23.cloned.1.call-done = f32[128,2048]{1,0:T(8,128)} async-done(((f32[1024,2048]{1,0:T(8,128)}), f32[128,2048]{1,0:T(8,128)}) %reduce-scatter.23.cloned.1.call-update) | async-done | bytes 1048592 | tf_op jit(solution)/shard_map/reduce_scatter | solution.py:229
  1535.2 120.1 %reduce-scatter.15.cloned.1.call-done = f32[2,128,2048]{2,1,0:T(8,128)} async-done(((f32[2,1024,2048]{2,1,0:T(8,128)}), f32[2,128,2048]{2,1,0:T(8,128)}) %reduce-scatter.15.cloned.1.call-update) | async-done | bytes 2097168 | tf_op jit(solution)/shard_map/reduce_scatter | solution.py:221
  (1036 shorter events, 587.1 us)
Async XLA Ops:
  7.2 60.5 %all-gather.9.cloned.1.call-start = ((), (), s32[]{:S(2)}) async-start(), calls=%async_computation.8 | async-start | bytes 2621440 | tf_op jit(solution)/shard_map/all_gather | solution.py:137
  7.9 105.5 %all-gather.11.cloned.1.call-start = ((), (), s32[]{:S(2)}) async-start(), calls=%async_computation.9 | async-start | bytes 9437184 | tf_op jit(solution)/shard_map/all_gather | solution.py:122
  8.7 152.3 %all-gather.15.cloned.1.call-start = ((), (), s32[]{:S(2)}) async-start(), calls=%async_computation.13 | async-start | bytes 2621440 | tf_op jit(solution)/shard_map/all_gather | solution.py:193
  9.4 188.8 %all-gather.13.cloned.1.call-start = ((), (), s32[]{:S(2)}) async-start(), calls=%async_computation.11 | async-start | bytes 4718592 | tf_op jit(solution)/shard_map/all_gather | solution.py:130
  10.0 238.8 %all-reduce.69.cloned.1.call-start = ((), (), s32[]{:S(2)}) async-start(), calls=%async_computation.10 | async-start | bytes 655360 | tf_op jit(solution)/shard_map/psum | solution.py:158
  41.0 80.1 %copy-start.102 = (f32[2048]{0:T(1024)}, f32[2048]{0:T(1024)S(1)}, u32[]{:S(2)}) copy-start(f32[2048]{0:T(1024)S(1)} %reshape.379) | copy-start | bytes 24580
  67.5 143.2 %copy-start.83 = (bf16[1024,160]{0,1:T(8,128)(2,1)}, bf16[1024,160]{0,1:T(8,128)(2,1)S(1)}, u32[]{:S(2)}) copy-start(bf16[1024,160]{0,1:T(8,128)(2,1)S(1)} %all_gather.45) | copy-start | bytes 983044
  67.5 130.6 %copy-start.115 = (f32[512]{0:T(512)}, f32[512]{0:T(512)S(1)}, u32[]{:S(2)}) copy-start(f32[512]{0:T(512)S(1)} %get-tuple-element.1111) | copy-start | bytes 6148
  67.6 130.6 %copy-start.116 = (f32[512]{0:T(512)}, f32[512]{0:T(512)S(1)}, u32[]{:S(2)}) copy-start(f32[512]{0:T(512)S(1)} %get-tuple-element.1112) | copy-start | bytes 6148
  67.6 130.6 %copy-start.117 = (f32[512]{0:T(512)}, f32[512]{0:T(512)S(1)}, u32[]{:S(2)}) copy-start(f32[512]{0:T(512)S(1)} %get-tuple-element.1113) | copy-start | bytes 6148
  67.6 130.6 %copy-start.107 = (f32[1024,1]{0,1:T(1,128)}, f32[1024,1]{0,1:T(1,128)S(1)}, u32[]{:S(2)}) copy-start(f32[1024,1]{0,1:T(1,128)S(1)} %get-tuple-element.1108) | copy-start | bytes 12292
  67.6 130.6 %copy-start.109 = (f32[1024,1]{0,1:T(1,128)}, f32[1024,1]{0,1:T(1,128)S(1)}, u32[]{:S(2)}) copy-start(f32[1024,1]{0,1:T(1,128)S(1)} %get-tuple-element.1110) | copy-start | bytes 12292
  67.6 130.6 %copy-start.111 = (f32[1024,1]{0,1:T(1,128)}, f32[1024,1]{0,1:T(1,128)S(1)}, u32[]{:S(2)}) copy-start(f32[1024,1]{0,1:T(1,128)S(1)} %get-tuple-element.1109) | copy-start | bytes 12292
  67.6 130.6 %copy-start.113 = (f32[1024,1]{0,1:T(1,128)}, f32[1024,1]{0,1:T(1,128)S(1)}, u32[]{:S(2)}) copy-start(f32[1024,1]{0,1:T(1,128)S(1)} %get-tuple-element.1107) | copy-start | bytes 12292
  70.0 51.1 %copy-start.120 = (f32[512]{0:T(512)}, f32[512]{0:T(512)S(1)}, u32[]{:S(2)}) copy-start(f32[512]{0:T(512)S(1)} %add_rsqrt_fusion) | copy-start | bytes 6148
  121.3 89.4 %copy-start.75 = (f32[509,1024]{1,0:T(8,128)}, f32[509,1024]{1,0:T(8,128)S(1)}, u32[]{:S(2)}) copy-start(f32[509,1024]{1,0:T(8,128)S(1)} %slice_bitcast_fusion.1) | copy-start | bytes 6254596
  198.2 23.1 %copy-start.123 = (bf16[128]{0:T(256)(128)(2,1)S(1)}, bf16[128]{0:T(256)(128)(2,1)}, u32[]{:S(2)}) copy-start(bf16[128]{0:T(256)(128)(2,1)} %param.36) | copy-start | bytes 772
  198.2 31.5 %copy-start.118 = (bf16[128,16]{0,1:T(8,128)(2,1)S(1)}, bf16[128,16]{0,1:T(8,128)(2,1)}, u32[]{:S(2)}) copy-start(bf16[128,16]{0,1:T(8,128)(2,1)} %param.35) | copy-start | bytes 12292
  198.2 40.3 %copy-start.105 = (bf16[128,128]{1,0:T(8,128)(2,1)S(1)}, bf16[128,128]{1,0:T(8,128)(2,1)}, u32[]{:S(2)}) copy-start(bf16[128,128]{1,0:T(8,128)(2,1)} %param.33) | copy-start | bytes 98308
  210.7 44.7 %copy-start.69 = (bf16[512,1024]{1,0:T(8,128)(2,1)}, bf16[512,1024]{1,0:T(8,128)(2,1)S(1)}, u32[]{:S(2)}) copy-start(bf16[512,1024]{1,0:T(8,128)(2,1)S(1)} %get-tuple-element.1055) | copy-start | bytes 3145732
  212.0 1023.5 %reduce-scatter.25.cloned.1.call-start = ((), (), s32[]{:S(2)}) async-start(), calls=%async_computation.20 | async-start | bytes 589824
  221.3 34.2 %copy-start.106 = (f32[8,1,128]{2,1,0:T(1,128)}, f32[8,1,128]{2,1,0:T(1,128)S(1)}, u32[]{:S(2)}) copy-start(f32[8,1,128]{2,1,0:T(1,128)S(1)} %convert_element_type.124) | copy-start | bytes 12292
  255.4 246.5 %copy-start.81 = (f32[1024,16]{0,1:T(8,128)S(1)}, f32[1024,16]{0,1:T(8,128)}, u32[]{:S(2)}) copy-start(f32[1024,16]{0,1:T(8,128)} %get-tuple-element.1815) | copy-start | bytes 196612
  578.4 28.0 %slice-start = ((s8[16777216]{0:T(1024)(128)(4,1)}), s8[4194304]{0:T(1024)(128)(4,1)S(1)}, s32[]{:S(2)}) async-start(s8[16777216]{0:T(1024)(128)(4,1)} %bitcast.492), calls=%async_computation.21 | async-start | bytes 8388608 | tf_op jit(solution)/shard_map/transpose(jvp())/while
  578.4 28.0 %slice-start.1 = ((s8[16777216]{0:T(1024)(128)(4,1)}), s8[4194304]{0:T(1024)(128)(4,1)S(1)}, s32[]{:S(2)}) async-start(s8[16777216]{0:T(1024)(128)(4,1)} %bitcast.492), calls=%async_computation.22 | async-start | bytes 8388608 | tf_op jit(solution)/shard_map/transpose(jvp())/while
  578.4 28.0 %slice-start.2 = ((s8[16777216]{0:T(1024)(128)(4,1)}), s8[4194304]{0:T(1024)(128)(4,1)S(1)}, s32[]{:S(2)}) async-start(s8[16777216]{0:T(1024)(128)(4,1)} %bitcast.492), calls=%async_computation.23 | async-start | bytes 8388608 | tf_op jit(solution)/shard_map/transpose(jvp())/while
  588.1 23.3 %copy-start.5 = (f32[16,1,1024,16]{2,3,0,1:T(8,128)S(1)}, f32[16,1,1024,16]{2,3,0,1:T(8,128)}, u32[]{:S(2)}) copy-start(f32[16,1,1024,16]{2,3,0,1:T(8,128)} %copy-done.4) | copy-start | bytes 3145732 | tf_op jit(solution)/shard_map/transpose(jvp())/while
  721.2 24.1 %copy-start.30 = (f32[16,1,1024,16]{2,3,0,1:T(8,128)}, f32[16,1,1024,16]{2,3,0,1:T(8,128)S(1)}, u32[]{:S(2)}) copy-start(f32[16,1,1024,16]{2,3,0,1:T(8,128)S(1)} %get-tuple-element.1646) | copy-start | bytes 3145732 | tf_op jit(solution)/shard_map/transpose(jvp())/while
  721.2 24.1 %copy-start.31 = (f32[16,1,1024,16]{2,3,0,1:T(8,128)}, f32[16,1,1024,16]{2,3,0,1:T(8,128)S(1)}, u32[]{:S(2)}) copy-start(f32[16,1,1024,16]{2,3,0,1:T(8,128)S(1)} %get-tuple-element.1648) | copy-start | bytes 3145732 | tf_op jit(solution)/shard_map/transpose(jvp())/while
  721.3 24.0 %copy-start.17 = (f32[16,1,1024,16]{2,3,0,1:T(8,128)S(1)}, f32[16,1,1024,16]{2,3,0,1:T(8,128)}, u32[]{:S(2)}) copy-start(f32[16,1,1024,16]{2,3,0,1:T(8,128)} %copy-done.16) | copy-start | bytes 3145732 | tf_op jit(solution)/shard_map/transpose(jvp())/while
  721.3 24.0 %copy-start.34 = (f32[16,1,1024,16]{2,3,0,1:T(8,128)S(1)}, f32[16,1,1024,16]{2,3,0,1:T(8,128)}, u32[]{:S(2)}) copy-start(f32[16,1,1024,16]{2,3,0,1:T(8,128)} %get-tuple-element.1656) | copy-start | bytes 3145732 | tf_op jit(solution)/shard_map/transpose(jvp())/while
  721.3 25.1 %copy-start.6 = (f32[16,1,1024,16]{2,3,0,1:T(8,128)S(1)}, f32[16,1,1024,16]{2,3,0,1:T(8,128)}, u32[]{:S(2)}) copy-start(f32[16,1,1024,16]{2,3,0,1:T(8,128)} %copy-done.4) | copy-start | bytes 3145732 | tf_op jit(solution)/shard_map/transpose(jvp())/while
  721.3 25.1 %copy-start.33 = (f32[16,1,1024,16]{2,3,0,1:T(8,128)S(1)}, f32[16,1,1024,16]{2,3,0,1:T(8,128)}, u32[]{:S(2)}) copy-start(f32[16,1,1024,16]{2,3,0,1:T(8,128)} %get-tuple-element.1654) | copy-start | bytes 3145732 | tf_op jit(solution)/shard_map/transpose(jvp())/while
  721.3 26.3 %copy-start.32 = (f32[16,1,1024,16]{2,3,0,1:T(8,128)S(1)}, f32[16,1,1024,16]{2,3,0,1:T(8,128)}, u32[]{:S(2)}) copy-start(f32[16,1,1024,16]{2,3,0,1:T(8,128)} %get-tuple-element.1652) | copy-start | bytes 3145732 | tf_op jit(solution)/shard_map/transpose(jvp())/while
  721.3 41.9 %slice-start.12 = ((s8[16777216]{0:T(1024)(128)(4,1)}), s8[4194304]{0:T(1024)(128)(4,1)S(1)}, s32[]{:S(2)}) async-start(s8[16777216]{0:T(1024)(128)(4,1)} %bitcast.498), calls=%async_computation.33 | async-start | bytes 8388608 | tf_op jit(solution)/shard_map/transpose(jvp())/while
  721.4 41.9 %slice-start.13 = ((s8[16777216]{0:T(1024)(128)(4,1)}), s8[4194304]{0:T(1024)(128)(4,1)S(1)}, s32[]{:S(2)}) async-start(s8[16777216]{0:T(1024)(128)(4,1)} %bitcast.498), calls=%async_computation.34 | async-start | bytes 8388608 | tf_op jit(solution)/shard_map/transpose(jvp())/while
  732.4 22.0 %copy-start.45 = (f32[16,1,1024,16]{2,3,0,1:T(8,128)S(1)}, f32[16,1,1024,16]{2,3,0,1:T(8,128)}, u32[]{:S(2)}) copy-start(f32[16,1,1024,16]{2,3,0,1:T(8,128)} %copy-done.44) | copy-start | bytes 3145732 | tf_op jit(solution)/shard_map/transpose(jvp())/while
  737.7 22.0 %copy-start.39 = (f32[16,1,1024,16]{2,3,0,1:T(8,128)S(1)}, f32[16,1,1024,16]{2,3,0,1:T(8,128)}, u32[]{:S(2)}) copy-start(f32[16,1,1024,16]{2,3,0,1:T(8,128)} %copy-done.38) | copy-start | bytes 3145732 | tf_op jit(solution)/shard_map/transpose(jvp())/while
  867.5 28.0 %slice-start = ((s8[16777216]{0:T(1024)(128)(4,1)}), s8[4194304]{0:T(1024)(128)(4,1)S(1)}, s32[]{:S(2)}) async-start(s8[16777216]{0:T(1024)(128)(4,1)} %bitcast.492), calls=%async_computation.21 | async-start | bytes 8388608 | tf_op jit(solution)/shard_map/transpose(jvp())/while
  867.5 28.0 %slice-start.1 = ((s8[16777216]{0:T(1024)(128)(4,1)}), s8[4194304]{0:T(1024)(128)(4,1)S(1)}, s32[]{:S(2)}) async-start(s8[16777216]{0:T(1024)(128)(4,1)} %bitcast.492), calls=%async_computation.22 | async-start | bytes 8388608 | tf_op jit(solution)/shard_map/transpose(jvp())/while
  867.5 28.0 %slice-start.2 = ((s8[16777216]{0:T(1024)(128)(4,1)}), s8[4194304]{0:T(1024)(128)(4,1)S(1)}, s32[]{:S(2)}) async-start(s8[16777216]{0:T(1024)(128)(4,1)} %bitcast.492), calls=%async_computation.23 | async-start | bytes 8388608 | tf_op jit(solution)/shard_map/transpose(jvp())/while
  877.1 23.3 %copy-start.5 = (f32[16,1,1024,16]{2,3,0,1:T(8,128)S(1)}, f32[16,1,1024,16]{2,3,0,1:T(8,128)}, u32[]{:S(2)}) copy-start(f32[16,1,1024,16]{2,3,0,1:T(8,128)} %copy-done.4) | copy-start | bytes 3145732 | tf_op jit(solution)/shard_map/transpose(jvp())/while
  1010.3 24.1 %copy-start.30 = (f32[16,1,1024,16]{2,3,0,1:T(8,128)}, f32[16,1,1024,16]{2,3,0,1:T(8,128)S(1)}, u32[]{:S(2)}) copy-start(f32[16,1,1024,16]{2,3,0,1:T(8,128)S(1)} %get-tuple-element.1646) | copy-start | bytes 3145732 | tf_op jit(solution)/shard_map/transpose(jvp())/while
  1010.3 24.1 %copy-start.31 = (f32[16,1,1024,16]{2,3,0,1:T(8,128)}, f32[16,1,1024,16]{2,3,0,1:T(8,128)S(1)}, u32[]{:S(2)}) copy-start(f32[16,1,1024,16]{2,3,0,1:T(8,128)S(1)} %get-tuple-element.1648) | copy-start | bytes 3145732 | tf_op jit(solution)/shard_map/transpose(jvp())/while
  1010.4 24.0 %copy-start.17 = (f32[16,1,1024,16]{2,3,0,1:T(8,128)S(1)}, f32[16,1,1024,16]{2,3,0,1:T(8,128)}, u32[]{:S(2)}) copy-start(f32[16,1,1024,16]{2,3,0,1:T(8,128)} %copy-done.16) | copy-start | bytes 3145732 | tf_op jit(solution)/shard_map/transpose(jvp())/while
  1010.4 24.0 %copy-start.34 = (f32[16,1,1024,16]{2,3,0,1:T(8,128)S(1)}, f32[16,1,1024,16]{2,3,0,1:T(8,128)}, u32[]{:S(2)}) copy-start(f32[16,1,1024,16]{2,3,0,1:T(8,128)} %get-tuple-element.1656) | copy-start | bytes 3145732 | tf_op jit(solution)/shard_map/transpose(jvp())/while
  1010.4 25.1 %copy-start.6 = (f32[16,1,1024,16]{2,3,0,1:T(8,128)S(1)}, f32[16,1,1024,16]{2,3,0,1:T(8,128)}, u32[]{:S(2)}) copy-start(f32[16,1,1024,16]{2,3,0,1:T(8,128)} %copy-done.4) | copy-start | bytes 3145732 | tf_op jit(solution)/shard_map/transpose(jvp())/while
  1010.4 25.1 %copy-start.33 = (f32[16,1,1024,16]{2,3,0,1:T(8,128)S(1)}, f32[16,1,1024,16]{2,3,0,1:T(8,128)}, u32[]{:S(2)}) copy-start(f32[16,1,1024,16]{2,3,0,1:T(8,128)} %get-tuple-element.1654) | copy-start | bytes 3145732 | tf_op jit(solution)/shard_map/transpose(jvp())/while
  1010.4 26.3 %copy-start.32 = (f32[16,1,1024,16]{2,3,0,1:T(8,128)S(1)}, f32[16,1,1024,16]{2,3,0,1:T(8,128)}, u32[]{:S(2)}) copy-start(f32[16,1,1024,16]{2,3,0,1:T(8,128)} %get-tuple-element.1652) | copy-start | bytes 3145732 | tf_op jit(solution)/shard_map/transpose(jvp())/while
  1010.4 41.9 %slice-start.12 = ((s8[16777216]{0:T(1024)(128)(4,1)}), s8[4194304]{0:T(1024)(128)(4,1)S(1)}, s32[]{:S(2)}) async-start(s8[16777216]{0:T(1024)(128)(4,1)} %bitcast.498), calls=%async_computation.33 | async-start | bytes 8388608 | tf_op jit(solution)/shard_map/transpose(jvp())/while
  1010.4 41.9 %slice-start.13 = ((s8[16777216]{0:T(1024)(128)(4,1)}), s8[4194304]{0:T(1024)(128)(4,1)S(1)}, s32[]{:S(2)}) async-start(s8[16777216]{0:T(1024)(128)(4,1)} %bitcast.498), calls=%async_computation.34 | async-start | bytes 8388608 | tf_op jit(solution)/shard_map/transpose(jvp())/while
  1021.5 22.0 %copy-start.45 = (f32[16,1,1024,16]{2,3,0,1:T(8,128)S(1)}, f32[16,1,1024,16]{2,3,0,1:T(8,128)}, u32[]{:S(2)}) copy-start(f32[16,1,1024,16]{2,3,0,1:T(8,128)} %copy-done.44) | copy-start | bytes 3145732 | tf_op jit(solution)/shard_map/transpose(jvp())/while
  1111.0 39.2 %copy-start.112 = (f32[1024,1]{0,1:T(1,128)S(1)}, f32[1024,1]{0,1:T(1,128)}, u32[]{:S(2)}) copy-start(f32[1024,1]{0,1:T(1,128)} %copy-done.111) | copy-start | bytes 12292
  1111.0 39.6 %copy-start.110 = (f32[1024,1]{0,1:T(1,128)S(1)}, f32[1024,1]{0,1:T(1,128)}, u32[]{:S(2)}) copy-start(f32[1024,1]{0,1:T(1,128)} %copy-done.109) | copy-start | bytes 12292
  1115.0 36.0 %copy-start.108 = (f32[1024,1]{0,1:T(1,128)S(1)}, f32[1024,1]{0,1:T(1,128)}, u32[]{:S(2)}) copy-start(f32[1024,1]{0,1:T(1,128)} %copy-done.107) | copy-start | bytes 12292
  1156.8 111.3 %reduce-scatter.13.cloned.1.call-start = ((), (), s32[]{:S(2)}) async-start(), calls=%async_computation.14 | async-start | bytes 5242880 | tf_op jit(solution)/shard_map/reduce_scatter | solution.py:215
  1168.1 179.4 %reduce-scatter.11.cloned.1.call-start = ((), (), s32[]{:S(2)}) async-start(), calls=%async_computation.12 | async-start | bytes 5242880 | tf_op jit(solution)/shard_map/reduce_scatter | solution.py:186
  1175.0 208.3 %reduce-scatter.21.cloned.1.call-start = ((), (), s32[]{:S(2)}) async-start(), calls=%async_computation.18 | async-start | bytes 73728 | tf_op jit(solution)/shard_map/reduce_scatter | solution.py:227
  1175.8 245.2 %reduce-scatter.19.cloned.1.call-start = ((), (), s32[]{:S(2)}) async-start(), calls=%async_computation.17 | async-start | bytes 589824 | tf_op jit(solution)/shard_map/reduce_scatter | solution.py:225
  1177.2 282.5 %reduce-scatter.17.cloned.1.call-start = ((), (), s32[]{:S(2)}) async-start(), calls=%async_computation.16 | async-start | bytes 737280 | tf_op jit(solution)/shard_map/reduce_scatter | solution.py:224
  1178.6 356.6 %reduce-scatter.23.cloned.1.call-start = ((), (), s32[]{:S(2)}) async-start(), calls=%async_computation.19 | async-start | bytes 9437184 | tf_op jit(solution)/shard_map/reduce_scatter | solution.py:229
  1186.5 468.9 %reduce-scatter.15.cloned.1.call-start = ((), (), s32[]{:S(2)}) async-start(), calls=%async_computation.15 | async-start | bytes 18874368 | tf_op jit(solution)/shard_map/reduce_scatter | solution.py:221
  1196.0 72.0 %copy-start.82 = (bf16[128,2048]{1,0:T(8,128)(2,1)S(1)}, bf16[128,2048]{1,0:T(8,128)(2,1)}, u32[]{:S(2)}) copy-start(bf16[128,2048]{1,0:T(8,128)(2,1)} %param.24) | copy-start | bytes 1572868
  1196.0 151.5 %copy-start.88 = (bf16[128,2048]{1,0:T(8,128)(2,1)S(1)}, bf16[128,2048]{1,0:T(8,128)(2,1)}, u32[]{:S(2)}) copy-start(bf16[128,2048]{1,0:T(8,128)(2,1)} %param.25) | copy-start | bytes 1572868
  (189 other events, 2349.9 us)
Sparse Core Ops, SparseCore 0:
  9.6 48.7 all-gather.8
  60.3 53.0 all-gather.10
  115.0 45.9 all-gather.14
  162.7 35.4 all-gather.12
  212.1 36.2 all-reduce.68
  1156.9 31.4 reduce-scatter.24
  1190.8 77.2 reduce-scatter.12
  1270.3 77.1 reduce-scatter.10
  1351.4 31.9 reduce-scatter.20
  1386.9 34.1 reduce-scatter.18
  1425.0 34.5 reduce-scatter.16
  1463.9 71.2 reduce-scatter.22
  1539.4 115.9 reduce-scatter.14
where the time goes:
time: 1680 us; the launch traced here: 1660 us
  other arithmetic  657 us (39%)
  waiting for transfers between devices  533 us (32%)
  local copies, waits for them, and re-layouts  187 us (11%)
  blocking collectives  147 us (9%)
  matrix products  71.2 us (4%)
  loops' own time  48.6 us (3%)
  between operations  17.3 us (1%)
    while x86, other arithmetic  135 us
    reduce_scatter x1, waiting for transfers between devices, shards(): lax.psum_scatter(w_in_grad, 'fsdp', scatter_dimension=1, tiled=True)  120 us
    while x432, local copies, waits for them, and re-layouts  96.3 us
    mul x20, other arithmetic, block_scan(): product = factors[:, offset] * product  84 us
    reduce_scatter x1, waiting for transfers between devices, shards(): lax.psum_scatter(jnp.dot(gated_low, w_out_t, preferred_element_type=f32),...  78 us
    reduce_scatter x1, waiting for transfers between devices, shards(): lax.psum_scatter(out_grad, 'fsdp', scatter_dimension=0, tiled=True)  75.6 us
    add x64, other arithmetic, carry_step(): return (members[0] * current + members[1], current)  57.8 us
    mul x28, other arithmetic, block_scan(): running = factors[:, offset] * running + drives[:, offset]  55.4 us
  transfers between devices with their start and end apart: 13, of which 10 were waited for; matrix products, arithmetic and copies ran while one was open for 4% of the time, Pallas kernels for 0%

commit v1 on v0

--- a/solution.py
+++ b/solution.py
@@ -190,7 +190,9 @@
         tiled=True,
     )
     output = (hidden.astype(f32) + branch).astype(bf16)
-    cot_all = lax.all_gather(cotangent, "tensor", axis=0, tiled=True)
+    cot_all = jnp.concatenate(
+        lax.all_to_all(jnp.stack([cotangent] * lax.axis_size("tensor")), "tensor", 0, 0), axis=0
+    )
     grad_gated = (
         jnp.einsum("gd,cd->gc", cot_all, w_out_t, preferred_element_type=f32)
         .astype(bf16)

time: 1680 us -> 1670 us (level)
  waiting for transfers between devices: 533 us -> 460 us
  blocking collectives: 147 us -> 205 us
    all_gather x1, blocking collectives: 12.4 us -> 69.2 us  [shards(): lax.all_gather(gain_fsdp, 'tensor', axis=0, tiled=True)]
    all_gather x1 -> x0, waiting for transfers between devices: 35.7 us -> none  [shards(): cot_all = lax.all_gather(cotangent, 'tensor', axis=0, tiled=True)]
    all_gather x1, waiting for transfers between devices: 43.4 us -> 18 us  [shards(): lax.all_gather(w_in, 'fsdp', axis=1, tiled=True)]
  transfers between devices with their start and end apart: 13 -> 13, of which waited for: 10 -> 9; matrix products, arithmetic and copies ran while one was open for 4% -> 4% of each run, Pallas kernels for 0% -> 0%
where the time goes in v1:
time: 1670 us; the launch traced here: 1660 us
  other arithmetic  657 us (39%)
  waiting for transfers between devices  460 us (28%)
  blocking collectives  205 us (12%)
  local copies, waits for them, and re-layouts  190 us (11%)
  matrix products  71.3 us (4%)
  loops' own time  48.6 us (3%)
  between operations  17.6 us (1%)
    while x86, other arithmetic  135 us
    reduce_scatter x1, waiting for transfers between devices, shards(): lax.psum_scatter(w_in_grad, 'fsdp', scatter_dimension=1, tiled=True)  120 us
    while x432, local copies, waits for them, and re-layouts  96.3 us
    mul x20, other arithmetic, block_scan(): product = factors[:, offset] * product  84 us
    reduce_scatter x1, waiting for transfers between devices, shards(): lax.psum_scatter(jnp.dot(gated_low, w_out_t, preferred_element_type=f32),...  77.8 us
    reduce_scatter x1, waiting for transfers between devices, shards(): lax.psum_scatter(out_grad, 'fsdp', scatter_dimension=0, tiled=True)  75.8 us
    all_gather x1, blocking collectives, shards(): lax.all_gather(gain_fsdp, 'tensor', axis=0, tiled=True)  69.2 us
    add x64, other arithmetic, carry_step(): return (members[0] * current + members[1], current)  57.8 us
  transfers between devices with their start and end apart: 13, of which 9 were waited for; matrix products, arithmetic and copies ran while one was open for 4% of the time, Pallas kernels for 0%

profile of v1, /device:TPU:0, one launch (start us, length us, event | category | flops | bytes accessed | tf_op | source)
XLA Modules:
  0.0 1656.3 jit_solution(11614225083900799068)
XLA Ops:
  12.0 6.3 all-to-all-start
  21.2 14.2 all-reduce.59
  36.4 69.2 %all-gather.1 = bf16[4,1,512]{2,1,0:T(2,128)(2,1)S(1)} all-gather(bf16[1,1,512]{2,1,0:T(2,128)(2,1)S(1)} %reshape.412), channel_id=1, replica_groups=mesh['fsdp'=8,'tensor'=4] {'tensor'}, dimensions={0}, use_global_device_ids=true | all-gather | bytes 5120 | tf_op jit(solution)/shard_map/all_gather | solution.py:138
  105.9 8.9 all-gather
  114.7 8.8 all_gather.37
  123.5 9.9 all_gather.42
  135.7 18.0 %all-gather.10.cloned.1.call-done = bf16[2,1024,2048]{2,1,0:T(8,128)(2,1)} async-done(((bf16[2,128,2048]{2,1,0:T(8,128)(2,1)}), bf16[2,1024,2048]{2,1,0:T(8,128)(2,1)}) %all-gather.10.cloned.1.call-update) | async-done | bytes 8388624 | tf_op jit(solution)/shard_map/all_gather | solution.py:122
  153.7 7.7 fusion.64
  165.5 25.9 %all-gather.12.cloned.1.call-done = bf16[1024,2048]{1,0:T(8,128)(2,1)} async-done(((bf16[128,2048]{1,0:T(8,128)(2,1)}), bf16[1024,2048]{1,0:T(8,128)(2,1)}) %all-gather.12.cloned.1.call-update) | async-done | bytes 4194320 | tf_op jit(solution)/shard_map/all_gather | solution.py:130
  191.5 12.5 multiply_reduce_fusion.6
  205.8 8.7 all-gather.2
  214.5 7.8 all-gather.3
  222.9 8.8 all_gather.45
  231.8 9.3 all_gather.43
  248.7 242.5 %while.116 = (s32[]{:T(128)}, f32[1024,16]{0,1:T(8,128)S(1)}, f32[2,256,1024]{2,1,0:T(8,128)}, f32[2,1024,16]{1,2,0:T(8,128)}, f32[2,256,1024]{2,1,0:T(8,128)}, ...) while((s32[]{:T(128)}, f32[1024,16]{0,1:T(8,128)S(1)}, ...), condition=%wide.region_9.10_spmd, body=%wide.region_5.9_spmd.sunk | while | flops 52199424 | bytes 568369280 | solution.py:83
  275.4 5.8 copy-done.3
  283.3 8.5 broadcast_multiply_fusion.10
  327.9 6.3 bitcast_add_fusion.23
  336.1 24.8 %while.120 = (s32[]{:T(128)}, f32[1024,16]{0,1:T(8,128)S(1)}, f32[16,1024,16]{1,2,0:T(8,128)}, f32[16,1024,16]{1,2,0:T(8,128)}, f32[16,1024,16]{1,2,0:T(8,128)}, /*index=5*/s32[]{:T(128)}) while((s32[]{:T(128)}, f32[1024,16]{0,1:T(8,128)S(1)}, f32[16,1024,16]{1,2,0:T(8,128)}, f32[16,1024,16]{1,2,0:T(8,128)}, f32[16,1024,16]{1,2,0:T(8,128)}, ...), condition=%wide.region_7.7_spmd, body=%wide.region_6.6_spmd.sunk | while | flops 32770 | bytes 393801 | solution.py:62
  361.1 12.8 multiply_reduce_fusion.15
  389.9 5.8 copy-done.3
  397.7 8.5 broadcast_multiply_fusion.10
  442.3 6.3 bitcast_add_fusion.23
  450.5 24.8 %while.120 = (s32[]{:T(128)}, f32[1024,16]{0,1:T(8,128)S(1)}, f32[16,1024,16]{1,2,0:T(8,128)}, f32[16,1024,16]{1,2,0:T(8,128)}, f32[16,1024,16]{1,2,0:T(8,128)}, /*index=5*/s32[]{:T(128)}) while((s32[]{:T(128)}, f32[1024,16]{0,1:T(8,128)S(1)}, f32[16,1024,16]{1,2,0:T(8,128)}, f32[16,1024,16]{1,2,0:T(8,128)}, f32[16,1024,16]{1,2,0:T(8,128)}, ...), condition=%wide.region_7.7_spmd, body=%wide.region_6.6_spmd.sunk | while | flops 32770 | bytes 393801 | solution.py:62
  475.6 12.8 multiply_reduce_fusion.15
  495.6 609.4 %while.119 = (s32[]{:T(128)}, f32[1024,16]{0,1:T(8,128)}, f32[1024,16]{0,1:T(8,128)S(1)}, f32[2,256,1024]{2,1,0:T(8,128)}, f32[2,256,1024]{2,1,0:T(8,128)}, /*in...) while((s32[]{:T(128)}, f32[1024,16]{0,1:T(8,128)}, ...), condition=%wide.region_22.23_spmd.clone, body=%wide.region_11.22_spmd.clone.sunk | while | flops 338518016 | bytes 1045472448 | solution.py:83
  527.1 7.1 broadcast_multiply_fusion.11
  535.0 6.5 fusion.145
  541.5 13.2 bitcast_add_fusion.24
  572.1 9.7 fusion.146
  628.2 15.0 while.121
  645.3 13.3 multiply_reduce_fusion.16
  659.8 24.9 %while.122 = (s32[]{:T(128)}, f32[1024,16]{0,1:T(8,128)S(1)}, f32[16,1024,16]{1,2,0:T(8,128)S(1)}, f32[16,1024,16]{1,2,0:T(8,128)}, f32[16,1024,16]{1,2,0:T(8,12...) while((s32[]{:T(128)}, f32[1024,16]{0,1:T(8,128)S(1)}, ...), condition=%wide.region_16.16_spmd, body=%wide.region_15.15_spmd.sunk | while | flops 49155 | bytes 524401 | solution.py:62
  684.7 7.6 multiply_add_fusion.26
  692.3 5.7 copy-done.2
  699.5 15.5 slice_add_fusion.81
  715.2 11.0 multiply_reduce_fusion.18
  787.6 14.9 multiply_reduce_fusion.17
  816.4 7.1 broadcast_multiply_fusion.11
  824.3 6.5 fusion.145
  830.8 13.2 bitcast_add_fusion.24
  861.4 9.7 fusion.146
  917.5 15.0 while.121
  934.6 13.3 multiply_reduce_fusion.16
  949.1 24.9 %while.122 = (s32[]{:T(128)}, f32[1024,16]{0,1:T(8,128)S(1)}, f32[16,1024,16]{1,2,0:T(8,128)S(1)}, f32[16,1024,16]{1,2,0:T(8,128)}, f32[16,1024,16]{1,2,0:T(8,12...) while((s32[]{:T(128)}, f32[1024,16]{0,1:T(8,128)S(1)}, ...), condition=%wide.region_16.16_spmd, body=%wide.region_15.15_spmd.sunk | while | flops 49155 | bytes 524401 | solution.py:62
  974.0 7.6 multiply_add_fusion.26
  988.8 15.5 slice_add_fusion.81
  1004.5 11.0 multiply_reduce_fusion.18
  1076.9 14.9 multiply_reduce_fusion.17
  1112.1 25.8 %all-reduce.70 = bf16[512,160]{0,1:T(8,128)(2,1)S(1)} all-reduce(f32[512,160]{0,1:T(8,128)S(1)} %pad_maximum_fusion.3), channel_id=1, replica_groups=mesh['fsdp'=8,'tensor'=4] {'tensor'}, use_global_device_ids=true, to_apply=%region_23.24 | all-reduce | flops 81920 | bytes 491520 | tf_op jit(solution)/shard_map/psum | solution.py:206
  1138.0 6.2 multiply_reduce_fusion.10
  1150.9 11.3 fusion.49
  1162.3 6.8 fusion.95
  1172.8 7.8 fusion.96
  1180.7 9.6 fusion.62
  1193.7 9.4 all-reduce.60
  1203.1 23.9 %all-reduce.65 = (f32[512]{0:T(512)S(1)}, f32[1024]{0:T(1024)S(1)}, f32[1024]{0:T(1024)S(1)}, f32[1024]{0:T(1024)S(1)}) all-reduce(f32[512]{0:T(512)S(1)} %dynamic-slice.2, f32[1024]{0:T(1024)S(1)} %get-tuple-element.866, f32[1024]{0:T(1024)S(1)} %get-tuple-element.1057, ...), channel_id=5, replica_groups=mesh['fsdp'=8,'tensor'=4] {'fsdp'}, use_global_device_ids=true, to_apply=%region_29.30.clone | all-reduce | flops 3584 | bytes 28672
  1230.9 31.1 %reduce-scatter.13.cloned.1.call-done = f32[128,2048]{1,0:T(8,128)} async-done(((f32[512,2048]{1,0:T(8,128)}), f32[128,2048]{1,0:T(8,128)}) %reduce-scatter.13.cloned.1.call-update) | async-done | bytes 1048592 | tf_op jit(solution)/shard_map/reduce_scatter | solution.py:217
  1263.6 77.8 %reduce-scatter.11.cloned.1.call-done = f32[128,2048]{1,0:T(8,128)} async-done(((f32[512,2048]{1,0:T(8,128)}), f32[128,2048]{1,0:T(8,128)}) %reduce-scatter.11.cloned.1.call-update) | async-done | bytes 1048592 | tf_op jit(solution)/shard_map/reduce_scatter | solution.py:186
  1344.5 32.7 %reduce-scatter.21.cloned.1.call-done = f32[128,16]{0,1:T(8,128)} async-done(((f32[1024,16]{0,1:T(8,128)}), f32[128,16]{0,1:T(8,128)}) %reduce-scatter.21.cloned.1.call-update) | async-done | bytes 8208 | tf_op jit(solution)/shard_map/reduce_scatter | solution.py:229
  1377.2 37.8 %reduce-scatter.19.cloned.1.call-done = f32[128,128]{1,0:T(8,128)} async-done(((f32[1024,128]{1,0:T(8,128)}), f32[128,128]{1,0:T(8,128)}) %reduce-scatter.19.cloned.1.call-update) | async-done | bytes 65552 | tf_op jit(solution)/shard_map/reduce_scatter | solution.py:227
  1415.0 38.4 %reduce-scatter.17.cloned.1.call-done = f32[128,160]{0,1:T(8,128)} async-done(((f32[1024,160]{0,1:T(8,128)}), f32[128,160]{0,1:T(8,128)}) %reduce-scatter.17.cloned.1.call-update) | async-done | bytes 81936 | tf_op jit(solution)/shard_map/reduce_scatter | solution.py:226
  1453.5 75.8 %reduce-scatter.23.cloned.1.call-done = f32[128,2048]{1,0:T(8,128)} async-done(((f32[1024,2048]{1,0:T(8,128)}), f32[128,2048]{1,0:T(8,128)}) %reduce-scatter.23.cloned.1.call-update) | async-done | bytes 1048592 | tf_op jit(solution)/shard_map/reduce_scatter | solution.py:231
  1529.2 120.0 %reduce-scatter.15.cloned.1.call-done = f32[2,128,2048]{2,1,0:T(8,128)} async-done(((f32[2,1024,2048]{2,1,0:T(8,128)}), f32[2,128,2048]{2,1,0:T(8,128)}) %reduce-scatter.15.cloned.1.call-update) | async-done | bytes 2097168 | tf_op jit(solution)/shard_map/reduce_scatter | solution.py:223
  (1036 shorter events, 589.6 us)
Async XLA Ops:
  7.2 126.4 %all-gather.8.cloned.1.call-start = ((), (), s32[]{:S(2)}) async-start(), calls=%async_computation.9 | async-start | bytes 2621440 | tf_op jit(solution)/shard_map/all_gather | solution.py:137
  7.9 145.8 %all-gather.10.cloned.1.call-start = ((), (), s32[]{:S(2)}) async-start(), calls=%async_computation.10 | async-start | bytes 9437184 | tf_op jit(solution)/shard_map/all_gather | solution.py:122
  8.7 182.7 %all-gather.12.cloned.1.call-start = ((), (), s32[]{:S(2)}) async-start(), calls=%async_computation.12 | async-start | bytes 4718592 | tf_op jit(solution)/shard_map/all_gather | solution.py:130
  12.0 153.5 %all-to-all-start = ((bf16[4,128,2048]{2,1,0:T(8,128)(2,1)}), bf16[4,128,2048]{2,1,0:T(8,128)(2,1)}, u32[]{:S(2)}, u32[]{:S(2)}) async-start(bf16[4,128,2048]{2,1,0:T(8,128)(2,1)} %stack.65), calls=%async_computation.1 | async-start | bytes 4194304 | tf_op jit(solution)/shard_map/all_to_all | solution.py:194
  18.3 223.7 %all-reduce.69.cloned.1.call-start = ((), (), s32[]{:S(2)}) async-start(), calls=%async_computation.11 | async-start | bytes 655360 | tf_op jit(solution)/shard_map/psum | solution.py:158
  105.9 55.5 %copy-start.102 = (f32[2048]{0:T(1024)}, f32[2048]{0:T(1024)S(1)}, u32[]{:S(2)}) copy-start(f32[2048]{0:T(1024)S(1)} %reshape.385) | copy-start | bytes 24580
  133.4 70.5 %copy-start.83 = (bf16[1024,160]{0,1:T(8,128)(2,1)}, bf16[1024,160]{0,1:T(8,128)(2,1)S(1)}, u32[]{:S(2)}) copy-start(bf16[1024,160]{0,1:T(8,128)(2,1)S(1)} %all_gather.42) | copy-start | bytes 983044
  133.4 58.0 %copy-start.115 = (f32[512]{0:T(512)}, f32[512]{0:T(512)S(1)}, u32[]{:S(2)}) copy-start(f32[512]{0:T(512)S(1)} %get-tuple-element.1111) | copy-start | bytes 6148
  133.4 58.0 %copy-start.116 = (f32[512]{0:T(512)}, f32[512]{0:T(512)S(1)}, u32[]{:S(2)}) copy-start(f32[512]{0:T(512)S(1)} %get-tuple-element.1112) | copy-start | bytes 6148
  133.4 58.0 %copy-start.117 = (f32[512]{0:T(512)}, f32[512]{0:T(512)S(1)}, u32[]{:S(2)}) copy-start(f32[512]{0:T(512)S(1)} %get-tuple-element.1113) | copy-start | bytes 6148
  133.5 57.9 %copy-start.107 = (f32[1024,1]{0,1:T(1,128)}, f32[1024,1]{0,1:T(1,128)S(1)}, u32[]{:S(2)}) copy-start(f32[1024,1]{0,1:T(1,128)S(1)} %get-tuple-element.1108) | copy-start | bytes 12292
  133.5 57.9 %copy-start.109 = (f32[1024,1]{0,1:T(1,128)}, f32[1024,1]{0,1:T(1,128)S(1)}, u32[]{:S(2)}) copy-start(f32[1024,1]{0,1:T(1,128)S(1)} %get-tuple-element.1110) | copy-start | bytes 12292
  133.5 57.9 %copy-start.111 = (f32[1024,1]{0,1:T(1,128)}, f32[1024,1]{0,1:T(1,128)S(1)}, u32[]{:S(2)}) copy-start(f32[1024,1]{0,1:T(1,128)S(1)} %get-tuple-element.1109) | copy-start | bytes 12292
  133.5 57.9 %copy-start.113 = (f32[1024,1]{0,1:T(1,128)}, f32[1024,1]{0,1:T(1,128)S(1)}, u32[]{:S(2)}) copy-start(f32[1024,1]{0,1:T(1,128)S(1)} %get-tuple-element.1107) | copy-start | bytes 12292
  135.7 25.7 %copy-start.120 = (f32[512]{0:T(512)}, f32[512]{0:T(512)S(1)}, u32[]{:S(2)}) copy-start(f32[512]{0:T(512)S(1)} %add_rsqrt_fusion) | copy-start | bytes 6148
  161.6 42.3 %copy-start.75 = (f32[509,1024]{1,0:T(8,128)}, f32[509,1024]{1,0:T(8,128)S(1)}, u32[]{:S(2)}) copy-start(f32[509,1024]{1,0:T(8,128)S(1)} %slice_bitcast_fusion.1) | copy-start | bytes 6254596
  191.5 23.1 %copy-start.123 = (bf16[128]{0:T(256)(128)(2,1)S(1)}, bf16[128]{0:T(256)(128)(2,1)}, u32[]{:S(2)}) copy-start(bf16[128]{0:T(256)(128)(2,1)} %param.36) | copy-start | bytes 772
  191.5 31.5 %copy-start.118 = (bf16[128,16]{0,1:T(8,128)(2,1)S(1)}, bf16[128,16]{0,1:T(8,128)(2,1)}, u32[]{:S(2)}) copy-start(bf16[128,16]{0,1:T(8,128)(2,1)} %param.35) | copy-start | bytes 12292
  191.5 40.3 %copy-start.105 = (bf16[128,128]{1,0:T(8,128)(2,1)S(1)}, bf16[128,128]{1,0:T(8,128)(2,1)}, u32[]{:S(2)}) copy-start(bf16[128,128]{1,0:T(8,128)(2,1)} %param.33) | copy-start | bytes 98308
  203.9 44.7 %copy-start.69 = (bf16[512,1024]{1,0:T(8,128)(2,1)}, bf16[512,1024]{1,0:T(8,128)(2,1)S(1)}, u32[]{:S(2)}) copy-start(bf16[512,1024]{1,0:T(8,128)(2,1)S(1)} %get-tuple-element.1055) | copy-start | bytes 3145732
  205.2 1024.2 %reduce-scatter.25.cloned.1.call-start = ((), (), s32[]{:S(2)}) async-start(), calls=%async_computation.20 | async-start | bytes 589824
  214.5 34.1 %copy-start.106 = (f32[8,1,128]{2,1,0:T(1,128)}, f32[8,1,128]{2,1,0:T(1,128)S(1)}, u32[]{:S(2)}) copy-start(f32[8,1,128]{2,1,0:T(1,128)S(1)} %convert_element_type.124) | copy-start | bytes 12292
  248.7 246.9 %copy-start.81 = (f32[1024,16]{0,1:T(8,128)S(1)}, f32[1024,16]{0,1:T(8,128)}, u32[]{:S(2)}) copy-start(f32[1024,16]{0,1:T(8,128)} %get-tuple-element.1815) | copy-start | bytes 196612
  572.1 28.0 %slice-start = ((s8[16777216]{0:T(1024)(128)(4,1)}), s8[4194304]{0:T(1024)(128)(4,1)S(1)}, s32[]{:S(2)}) async-start(s8[16777216]{0:T(1024)(128)(4,1)} %bitcast.493), calls=%async_computation.21 | async-start | bytes 8388608 | tf_op jit(solution)/shard_map/transpose(jvp())/while
  572.1 28.0 %slice-start.1 = ((s8[16777216]{0:T(1024)(128)(4,1)}), s8[4194304]{0:T(1024)(128)(4,1)S(1)}, s32[]{:S(2)}) async-start(s8[16777216]{0:T(1024)(128)(4,1)} %bitcast.493), calls=%async_computation.22 | async-start | bytes 8388608 | tf_op jit(solution)/shard_map/transpose(jvp())/while
  572.1 28.0 %slice-start.2 = ((s8[16777216]{0:T(1024)(128)(4,1)}), s8[4194304]{0:T(1024)(128)(4,1)S(1)}, s32[]{:S(2)}) async-start(s8[16777216]{0:T(1024)(128)(4,1)} %bitcast.493), calls=%async_computation.23 | async-start | bytes 8388608 | tf_op jit(solution)/shard_map/transpose(jvp())/while
  581.8 23.3 %copy-start.5 = (f32[16,1,1024,16]{2,3,0,1:T(8,128)S(1)}, f32[16,1,1024,16]{2,3,0,1:T(8,128)}, u32[]{:S(2)}) copy-start(f32[16,1,1024,16]{2,3,0,1:T(8,128)} %copy-done.4) | copy-start | bytes 3145732 | tf_op jit(solution)/shard_map/transpose(jvp())/while
  715.1 24.1 %copy-start.30 = (f32[16,1,1024,16]{2,3,0,1:T(8,128)}, f32[16,1,1024,16]{2,3,0,1:T(8,128)S(1)}, u32[]{:S(2)}) copy-start(f32[16,1,1024,16]{2,3,0,1:T(8,128)S(1)} %get-tuple-element.1646) | copy-start | bytes 3145732 | tf_op jit(solution)/shard_map/transpose(jvp())/while
  715.1 24.1 %copy-start.31 = (f32[16,1,1024,16]{2,3,0,1:T(8,128)}, f32[16,1,1024,16]{2,3,0,1:T(8,128)S(1)}, u32[]{:S(2)}) copy-start(f32[16,1,1024,16]{2,3,0,1:T(8,128)S(1)} %get-tuple-element.1648) | copy-start | bytes 3145732 | tf_op jit(solution)/shard_map/transpose(jvp())/while
  715.1 24.0 %copy-start.17 = (f32[16,1,1024,16]{2,3,0,1:T(8,128)S(1)}, f32[16,1,1024,16]{2,3,0,1:T(8,128)}, u32[]{:S(2)}) copy-start(f32[16,1,1024,16]{2,3,0,1:T(8,128)} %copy-done.16) | copy-start | bytes 3145732 | tf_op jit(solution)/shard_map/transpose(jvp())/while
  715.1 24.0 %copy-start.34 = (f32[16,1,1024,16]{2,3,0,1:T(8,128)S(1)}, f32[16,1,1024,16]{2,3,0,1:T(8,128)}, u32[]{:S(2)}) copy-start(f32[16,1,1024,16]{2,3,0,1:T(8,128)} %get-tuple-element.1656) | copy-start | bytes 3145732 | tf_op jit(solution)/shard_map/transpose(jvp())/while
  715.1 25.1 %copy-start.6 = (f32[16,1,1024,16]{2,3,0,1:T(8,128)S(1)}, f32[16,1,1024,16]{2,3,0,1:T(8,128)}, u32[]{:S(2)}) copy-start(f32[16,1,1024,16]{2,3,0,1:T(8,128)} %copy-done.4) | copy-start | bytes 3145732 | tf_op jit(solution)/shard_map/transpose(jvp())/while
  715.2 25.1 %copy-start.33 = (f32[16,1,1024,16]{2,3,0,1:T(8,128)S(1)}, f32[16,1,1024,16]{2,3,0,1:T(8,128)}, u32[]{:S(2)}) copy-start(f32[16,1,1024,16]{2,3,0,1:T(8,128)} %get-tuple-element.1654) | copy-start | bytes 3145732 | tf_op jit(solution)/shard_map/transpose(jvp())/while
  715.2 26.3 %copy-start.32 = (f32[16,1,1024,16]{2,3,0,1:T(8,128)S(1)}, f32[16,1,1024,16]{2,3,0,1:T(8,128)}, u32[]{:S(2)}) copy-start(f32[16,1,1024,16]{2,3,0,1:T(8,128)} %get-tuple-element.1652) | copy-start | bytes 3145732 | tf_op jit(solution)/shard_map/transpose(jvp())/while
  715.2 41.9 %slice-start.12 = ((s8[16777216]{0:T(1024)(128)(4,1)}), s8[4194304]{0:T(1024)(128)(4,1)S(1)}, s32[]{:S(2)}) async-start(s8[16777216]{0:T(1024)(128)(4,1)} %bitcast.499), calls=%async_computation.33 | async-start | bytes 8388608 | tf_op jit(solution)/shard_map/transpose(jvp())/while
  715.2 41.9 %slice-start.13 = ((s8[16777216]{0:T(1024)(128)(4,1)}), s8[4194304]{0:T(1024)(128)(4,1)S(1)}, s32[]{:S(2)}) async-start(s8[16777216]{0:T(1024)(128)(4,1)} %bitcast.499), calls=%async_computation.34 | async-start | bytes 8388608 | tf_op jit(solution)/shard_map/transpose(jvp())/while
  726.2 22.1 %copy-start.45 = (f32[16,1,1024,16]{2,3,0,1:T(8,128)S(1)}, f32[16,1,1024,16]{2,3,0,1:T(8,128)}, u32[]{:S(2)}) copy-start(f32[16,1,1024,16]{2,3,0,1:T(8,128)} %copy-done.44) | copy-start | bytes 3145732 | tf_op jit(solution)/shard_map/transpose(jvp())/while
  731.5 22.0 %copy-start.39 = (f32[16,1,1024,16]{2,3,0,1:T(8,128)S(1)}, f32[16,1,1024,16]{2,3,0,1:T(8,128)}, u32[]{:S(2)}) copy-start(f32[16,1,1024,16]{2,3,0,1:T(8,128)} %copy-done.38) | copy-start | bytes 3145732 | tf_op jit(solution)/shard_map/transpose(jvp())/while
  861.4 28.0 %slice-start = ((s8[16777216]{0:T(1024)(128)(4,1)}), s8[4194304]{0:T(1024)(128)(4,1)S(1)}, s32[]{:S(2)}) async-start(s8[16777216]{0:T(1024)(128)(4,1)} %bitcast.493), calls=%async_computation.21 | async-start | bytes 8388608 | tf_op jit(solution)/shard_map/transpose(jvp())/while
  861.4 28.0 %slice-start.1 = ((s8[16777216]{0:T(1024)(128)(4,1)}), s8[4194304]{0:T(1024)(128)(4,1)S(1)}, s32[]{:S(2)}) async-start(s8[16777216]{0:T(1024)(128)(4,1)} %bitcast.493), calls=%async_computation.22 | async-start | bytes 8388608 | tf_op jit(solution)/shard_map/transpose(jvp())/while
  861.4 28.0 %slice-start.2 = ((s8[16777216]{0:T(1024)(128)(4,1)}), s8[4194304]{0:T(1024)(128)(4,1)S(1)}, s32[]{:S(2)}) async-start(s8[16777216]{0:T(1024)(128)(4,1)} %bitcast.493), calls=%async_computation.23 | async-start | bytes 8388608 | tf_op jit(solution)/shard_map/transpose(jvp())/while
  871.1 23.3 %copy-start.5 = (f32[16,1,1024,16]{2,3,0,1:T(8,128)S(1)}, f32[16,1,1024,16]{2,3,0,1:T(8,128)}, u32[]{:S(2)}) copy-start(f32[16,1,1024,16]{2,3,0,1:T(8,128)} %copy-done.4) | copy-start | bytes 3145732 | tf_op jit(solution)/shard_map/transpose(jvp())/while
  1004.4 24.1 %copy-start.30 = (f32[16,1,1024,16]{2,3,0,1:T(8,128)}, f32[16,1,1024,16]{2,3,0,1:T(8,128)S(1)}, u32[]{:S(2)}) copy-start(f32[16,1,1024,16]{2,3,0,1:T(8,128)S(1)} %get-tuple-element.1646) | copy-start | bytes 3145732 | tf_op jit(solution)/shard_map/transpose(jvp())/while
  1004.4 24.1 %copy-start.31 = (f32[16,1,1024,16]{2,3,0,1:T(8,128)}, f32[16,1,1024,16]{2,3,0,1:T(8,128)S(1)}, u32[]{:S(2)}) copy-start(f32[16,1,1024,16]{2,3,0,1:T(8,128)S(1)} %get-tuple-element.1648) | copy-start | bytes 3145732 | tf_op jit(solution)/shard_map/transpose(jvp())/while
  1004.4 24.0 %copy-start.17 = (f32[16,1,1024,16]{2,3,0,1:T(8,128)S(1)}, f32[16,1,1024,16]{2,3,0,1:T(8,128)}, u32[]{:S(2)}) copy-start(f32[16,1,1024,16]{2,3,0,1:T(8,128)} %copy-done.16) | copy-start | bytes 3145732 | tf_op jit(solution)/shard_map/transpose(jvp())/while
  1004.4 24.0 %copy-start.34 = (f32[16,1,1024,16]{2,3,0,1:T(8,128)S(1)}, f32[16,1,1024,16]{2,3,0,1:T(8,128)}, u32[]{:S(2)}) copy-start(f32[16,1,1024,16]{2,3,0,1:T(8,128)} %get-tuple-element.1656) | copy-start | bytes 3145732 | tf_op jit(solution)/shard_map/transpose(jvp())/while
  1004.4 25.1 %copy-start.6 = (f32[16,1,1024,16]{2,3,0,1:T(8,128)S(1)}, f32[16,1,1024,16]{2,3,0,1:T(8,128)}, u32[]{:S(2)}) copy-start(f32[16,1,1024,16]{2,3,0,1:T(8,128)} %copy-done.4) | copy-start | bytes 3145732 | tf_op jit(solution)/shard_map/transpose(jvp())/while
  1004.4 25.1 %copy-start.33 = (f32[16,1,1024,16]{2,3,0,1:T(8,128)S(1)}, f32[16,1,1024,16]{2,3,0,1:T(8,128)}, u32[]{:S(2)}) copy-start(f32[16,1,1024,16]{2,3,0,1:T(8,128)} %get-tuple-element.1654) | copy-start | bytes 3145732 | tf_op jit(solution)/shard_map/transpose(jvp())/while
  1004.5 26.3 %copy-start.32 = (f32[16,1,1024,16]{2,3,0,1:T(8,128)S(1)}, f32[16,1,1024,16]{2,3,0,1:T(8,128)}, u32[]{:S(2)}) copy-start(f32[16,1,1024,16]{2,3,0,1:T(8,128)} %get-tuple-element.1652) | copy-start | bytes 3145732 | tf_op jit(solution)/shard_map/transpose(jvp())/while
  1004.5 41.9 %slice-start.12 = ((s8[16777216]{0:T(1024)(128)(4,1)}), s8[4194304]{0:T(1024)(128)(4,1)S(1)}, s32[]{:S(2)}) async-start(s8[16777216]{0:T(1024)(128)(4,1)} %bitcast.499), calls=%async_computation.33 | async-start | bytes 8388608 | tf_op jit(solution)/shard_map/transpose(jvp())/while
  1004.5 41.9 %slice-start.13 = ((s8[16777216]{0:T(1024)(128)(4,1)}), s8[4194304]{0:T(1024)(128)(4,1)S(1)}, s32[]{:S(2)}) async-start(s8[16777216]{0:T(1024)(128)(4,1)} %bitcast.499), calls=%async_computation.34 | async-start | bytes 8388608 | tf_op jit(solution)/shard_map/transpose(jvp())/while
  1015.5 22.1 %copy-start.45 = (f32[16,1,1024,16]{2,3,0,1:T(8,128)S(1)}, f32[16,1,1024,16]{2,3,0,1:T(8,128)}, u32[]{:S(2)}) copy-start(f32[16,1,1024,16]{2,3,0,1:T(8,128)} %copy-done.44) | copy-start | bytes 3145732 | tf_op jit(solution)/shard_map/transpose(jvp())/while
  1105.0 39.2 %copy-start.112 = (f32[1024,1]{0,1:T(1,128)S(1)}, f32[1024,1]{0,1:T(1,128)}, u32[]{:S(2)}) copy-start(f32[1024,1]{0,1:T(1,128)} %copy-done.111) | copy-start | bytes 12292
  1105.0 39.6 %copy-start.110 = (f32[1024,1]{0,1:T(1,128)S(1)}, f32[1024,1]{0,1:T(1,128)}, u32[]{:S(2)}) copy-start(f32[1024,1]{0,1:T(1,128)} %copy-done.109) | copy-start | bytes 12292
  1109.1 36.0 %copy-start.108 = (f32[1024,1]{0,1:T(1,128)S(1)}, f32[1024,1]{0,1:T(1,128)}, u32[]{:S(2)}) copy-start(f32[1024,1]{0,1:T(1,128)} %copy-done.107) | copy-start | bytes 12292
  1150.9 111.2 %reduce-scatter.13.cloned.1.call-start = ((), (), s32[]{:S(2)}) async-start(), calls=%async_computation.14 | async-start | bytes 5242880 | tf_op jit(solution)/shard_map/reduce_scatter | solution.py:217
  1162.2 179.2 %reduce-scatter.11.cloned.1.call-start = ((), (), s32[]{:S(2)}) async-start(), calls=%async_computation.13 | async-start | bytes 5242880 | tf_op jit(solution)/shard_map/reduce_scatter | solution.py:186
  1169.2 208.1 %reduce-scatter.21.cloned.1.call-start = ((), (), s32[]{:S(2)}) async-start(), calls=%async_computation.18 | async-start | bytes 73728 | tf_op jit(solution)/shard_map/reduce_scatter | solution.py:229
  1169.9 245.1 %reduce-scatter.19.cloned.1.call-start = ((), (), s32[]{:S(2)}) async-start(), calls=%async_computation.17 | async-start | bytes 589824 | tf_op jit(solution)/shard_map/reduce_scatter | solution.py:227
  1171.3 282.2 %reduce-scatter.17.cloned.1.call-start = ((), (), s32[]{:S(2)}) async-start(), calls=%async_computation.16 | async-start | bytes 737280 | tf_op jit(solution)/shard_map/reduce_scatter | solution.py:226
  1172.8 356.5 %reduce-scatter.23.cloned.1.call-start = ((), (), s32[]{:S(2)}) async-start(), calls=%async_computation.19 | async-start | bytes 9437184 | tf_op jit(solution)/shard_map/reduce_scatter | solution.py:231
  1180.6 468.7 %reduce-scatter.15.cloned.1.call-start = ((), (), s32[]{:S(2)}) async-start(), calls=%async_computation.15 | async-start | bytes 18874368 | tf_op jit(solution)/shard_map/reduce_scatter | solution.py:223
  1190.3 71.7 %copy-start.82 = (bf16[128,2048]{1,0:T(8,128)(2,1)S(1)}, bf16[128,2048]{1,0:T(8,128)(2,1)}, u32[]{:S(2)}) copy-start(bf16[128,2048]{1,0:T(8,128)(2,1)} %param.24) | copy-start | bytes 1572868
  1190.3 151.1 %copy-start.88 = (bf16[128,2048]{1,0:T(8,128)(2,1)S(1)}, bf16[128,2048]{1,0:T(8,128)(2,1)}, u32[]{:S(2)}) copy-start(bf16[128,2048]{1,0:T(8,128)(2,1)} %param.25) | copy-start | bytes 1572868
  (189 other events, 2350.7 us)
Sparse Core Ops, SparseCore 0:
  9.6 86.4 all-gather.7
  98.0 55.6 all-gather.9
  155.6 35.7 all-gather.11
  205.3 36.2 all-reduce.68
  1151.0 31.4 reduce-scatter.24
  1184.7 77.2 reduce-scatter.12
  1264.3 77.0 reduce-scatter.10
  1345.3 31.9 reduce-scatter.20
  1380.9 34.1 reduce-scatter.18
  1418.9 34.5 reduce-scatter.16
  1457.9 71.2 reduce-scatter.22
  1533.2 115.9 reduce-scatter.14
